TPU v7x, 32 devices: a whole 2x2x4 slice. The times are simulated.
32 devices in a mesh: slab: 8 (over y, x, core), grp: 4 (over z).
Axes of the slice: x: 2, y: 2, z: 4, core: 2. Of those that a mesh axis runs over, the one named last changes fastest.
Arguments:
- near_field: bfloat16 [2, 4096, 2048], P(None, 'slab', 'grp'), may hold values from -6 to 6
- lens_phase: float32 [2, 4096, 2048], P(None, 'slab', 'grp'), may hold values from -3.140625 to 3.140625
Outputs:
- far_field: float32 [2, 512, 2048], P(None, ('slab', 'grp'))
All inputs are finite; a program needn't handle non-finite values.
Results may differ from a plain program's by a relative error of at most 0.0083.
Values may be sent and summed in bfloat16 or wider, within the bound.
A program may use at most 128 MiB of HBM per device.

v0:
```python
import math
import jax
import jax.numpy as jnp
from jax import lax
from jax.sharding import PartitionSpec as P

AV = 512
AL = 2048
PHASE_CODE = 40.0


def sincos(angle):
    half = 0.5 * angle
    sq = half * half
    sin = -1.0 / 39916800.0
    for term in (1.0 / 362880.0, -1.0 / 5040.0, 1.0 / 120.0, -1.0 / 6.0, 1.0):
        sin = sin * sq + term
    sin = sin * half
    cos = 1.0 / 479001600.0
    for term in (-1.0 / 3628800.0, 1.0 / 40320.0, -1.0 / 720.0, 1.0 / 24.0, -0.5, 1.0):
        cos = cos * sq + term
    return (1.0 - 2.0 * sin * sin, 2.0 * sin * cos)


def unit_angle(turns, modulus):
    assert modulus & modulus - 1 == 0
    centred = (turns + modulus // 2 & modulus - 1) - modulus // 2
    return sincos(centred.astype(jnp.float32) * (2.0 * math.pi / modulus))


def count(size):
    return lax.optimization_barrier(jnp.arange(size, dtype=jnp.int32))


def phase_table(row_index, col_index, modulus):
    cos, sin = unit_angle(row_index[:, None] * col_index[None, :], modulus)
    return (cos.astype(jnp.bfloat16), sin.astype(jnp.bfloat16))


def propagator(points):
    band = math.gcd(points, 128)
    offset = count(points)[None, :] - count(band)[:, None]
    cos, sin = unit_angle(offset * offset - points // 4, 2 * points)
    gain = 1.0 / math.sqrt(points)

    def rolled(part):
        part = lax.optimization_barrier((part * gain).astype(jnp.bfloat16))
        twice = jnp.concatenate([part, part], axis=1)
        return jnp.concatenate(
            [
                lax.slice_in_dim(twice, points - start, 2 * points - start, axis=1)
                for start in range(0, points, band)
            ]
        )

    return (rolled(cos), rolled(sin))


def matmul(left, right):
    return jnp.dot(left, right, preferred_element_type=jnp.float32)


def complex_product(both, table_cos, table_sin):
    rows = both.shape[0] // 2
    with_cos = matmul(both, table_cos)
    with_sin = matmul(both, table_sin)
    return (with_cos[:rows] - with_sin[rows:], with_sin[:rows] + with_cos[rows:])


def on_device(near_field, lens_phase):
    slab_count = lax.axis_size("slab")
    group_count = lax.axis_size("grp")
    devices = slab_count * group_count
    steps, lat_dev, width = lens_phase.shape
    points = width * group_count
    total_rows = lat_dev * slab_count
    rows = lat_dev // group_count
    angles = AV // devices
    coded = [jnp.exp2(lens_phase[k] * PHASE_CODE).astype(jnp.bfloat16) for k in range(steps)]
    field = lax.all_to_all(near_field, "grp", split_axis=1, concat_axis=2, tiled=True)
    coded = [lax.all_to_all(part, "grp", split_axis=0, concat_axis=1, tiled=True) for part in coded]
    prop_cos, prop_sin = propagator(points)
    both = field.reshape(2 * rows, points)
    for section in range(steps):
        real, imag = complex_product(both, prop_cos, prop_sin)
        real = real.astype(jnp.bfloat16).astype(jnp.float32)
        imag = imag.astype(jnp.bfloat16).astype(jnp.float32)
        phase = jnp.log2(coded[section].astype(jnp.float32)) * (1.0 / PHASE_CODE)
        lens_cos, lens_sin = sincos(phase)
        both = jnp.concatenate(
            [
                (real * lens_cos - imag * lens_sin).astype(jnp.bfloat16),
                (real * lens_sin + imag * lens_cos).astype(jnp.bfloat16),
            ]
        )
    vert_cos, vert_sin = phase_table(count(points) - points // 2, count(AV) - AV // 2, 2 * points)
    col_real, col_imag = complex_product(both, vert_cos, -vert_sin)
    cols = jnp.stack([col_real, col_imag]).astype(jnp.bfloat16)
    cols = jnp.transpose(cols.reshape(2, rows, devices, angles), (2, 0, 3, 1))
    got = lax.all_to_all(cols, ("slab", "grp"), split_axis=0, concat_axis=0, tiled=True)
    modulus = 2 * total_rows
    period = modulus // rows
    source = count(devices) - devices // 2
    fine = count(period)
    near = count(rows)
    coarse = count(AL // period)
    w_cos, w_sin = phase_table(source, fine, period)
    got_real = got[:, 0]
    got_imag = got[:, 1]
    ein = lambda s, l, r: jnp.einsum(s, l, r, preferred_element_type=jnp.float32)
    mid_real = ein("sam,sf->afm", got_real, w_cos) + ein("sam,sf->afm", got_imag, w_sin)
    mid_imag = ein("sam,sf->afm", got_imag, w_cos) - ein("sam,sf->afm", got_real, w_sin)
    t_cos, t_sin = unit_angle(fine[:, None] * near[None, :], modulus)
    turned_real = (mid_real * t_cos + mid_imag * t_sin).astype(jnp.bfloat16)
    turned_imag = (mid_imag * t_cos - mid_real * t_sin).astype(jnp.bfloat16)
    e_cos, e_sin = phase_table(near, coarse * period - AL // 2, modulus)
    out_real = ein("afm,mc->acf", turned_real, e_cos) + ein("afm,mc->acf", turned_imag, e_sin)
    out_imag = ein("afm,mc->acf", turned_imag, e_cos) - ein("afm,mc->acf", turned_real, e_sin)
    scale = 1.0 / math.sqrt(total_rows * points)
    return (jnp.stack([out_real, out_imag]) * scale).reshape(2, angles, AL)


def solution(mesh):
    return jax.shard_map(
        on_device,
        mesh=mesh,
        in_specs=(P(None, "slab", "grp"), P(None, "slab", "grp")),
        out_specs=P(None, ("slab", "grp"), None),
        check_vma=False,
    )
```

profile of v0, /device:TPU:0, one launch (start us, length us, event | category | flops | bytes accessed | tf_op | source)
XLA Modules:
  0.0 123.4 jit_solution(17463661891979874556)
XLA Ops:
  0.0 2.8 %exponential_convert_fusion.1 = (bf16[1,512,512]{2,1,0:T(8,128)(2,1)}, bf16[1,512,512]{2,1,0:T(8,128)(2,1)}) fusion(f32[2,512,512]{2,1,0:T(8,128)} %param.3), kind=kLoop, calls=%fused_computation.138 | loop fusion | flops 1048576 | bytes 3145728 | tf_op jit(solution)/shard_map/convert_element_type | solution.py:79
  2.8 6.3 %all-to-all-start.1 = ((bf16[4,128,512]{2,1,0:T(8,128)(2,1)}), bf16[4,128,512]{2,1,0:T(8,128)(2,1)S(1)}, u32[]{:S(2)}, u32[]{:S(2)}) async-start(bf16[4,128,512]{2,1,0:T(8,128)(2,1)} %bitcast.6), calls=%async_computation.1 | async-start | bytes 1048576 | tf_op jit(solution)/shard_map/all_to_all | solution.py:81
  9.2 1.4 %fusion.27 = (bf16[128,2048]{1,0:T(8,128)(2,1)S(1)}, bf16[128,2048]{1,0:T(8,128)(2,1)S(1)}) fusion(s32[128]{0:T(128)S(1)} %iota.18, s32[2048]{0:T(1024)S(1)} %iota.21), kind=kLoop, calls=%fused_computation.108 | loop fusion | flops 10223616 | bytes 1057280 | tf_op jit(solution)/shard_map/convert_element_type | solution.py:47
  11.3 0.9 constant_dynamic-update-slice_fusion
  12.2 1.3 %fusion.76 = bf16[2048,2048]{1,0:T(8,128)(2,1)} fusion(bf16[2048,2048]{1,0:T(8,128)(2,1)} %constant_dynamic-update-slice_fusion, bf16[128,2048]{1,0:T(8,128)(2,1)S(1)} %get-tuple-element.20), kind=kLoop, calls=%fused_computation.180 | loop fusion | flops 1048576 | bytes 1048576
  13.6 0.8 fusion.78
  14.4 0.9 fusion.80
  16.1 0.8 fusion.84
  17.8 0.9 fusion.88
  18.6 0.9 fusion.90
  19.5 4.1 %all-to-all-done.1 = bf16[4,128,512]{2,1,0:T(8,128)(2,1)S(1)} async-done(((bf16[4,128,512]{2,1,0:T(8,128)(2,1)}), bf16[4,128,512]{2,1,0:T(8,128)(2,1)S(1)}, u32[]{:S(2)}, u32[]{:S(2)}) %all-to-all-start.1) | async-done | bytes 524320 | tf_op jit(solution)/shard_map/all_to_all | solution.py:81
  23.6 3.5 %all-to-all-start.2 = ((bf16[4,128,512]{2,1,0:T(8,128)(2,1)}), bf16[4,128,512]{2,1,0:T(8,128)(2,1)S(1)}, u32[]{:S(2)}, u32[]{:S(2)}) async-start(bf16[4,128,512]{2,1,0:T(8,128)(2,1)} %bitcast.8), calls=%async_computation.2 | async-start | bytes 1048576 | tf_op jit(solution)/shard_map/all_to_all | solution.py:81
  27.1 2.1 %copy.14 = bf16[2,512,512]{2,0,1:T(2,128)(2,1)} copy(bf16[2,512,512]{2,1,0:T(8,128)(2,1)S(1)} %copy-done.1) | data formatting | bytes 2097152 | tf_op args[0]
  30.1 0.9 fusion.94
  30.9 0.9 fusion.96
  31.8 9.4 %all-to-all-done.2 = bf16[4,128,512]{2,1,0:T(8,128)(2,1)S(1)} async-done(((bf16[4,128,512]{2,1,0:T(8,128)(2,1)}), bf16[4,128,512]{2,1,0:T(8,128)(2,1)S(1)}, u32[]{:S(2)}, u32[]{:S(2)}) %all-to-all-start.2) | async-done | bytes 524320 | tf_op jit(solution)/shard_map/all_to_all | solution.py:81
  41.1 3.7 %all-to-all-start = ((bf16[2,512,512]{2,0,1:T(2,128)(2,1)}), bf16[2,512,512]{2,0,1:T(2,128)(2,1)S(1)}, u32[]{:S(2)}, u32[]{:S(2)}) async-start(bf16[2,512,512]{2,0,1:T(2,128)(2,1)} %copy.14), calls=%async_computation | async-start | bytes 2097152 | tf_op jit(solution)/shard_map/all_to_all | solution.py:80
  45.7 0.8 fusion.100
  48.5 1.2 multiply_bitcast_fusion
  49.8 20.1 %all-to-all-done = bf16[2,512,512]{2,0,1:T(2,128)(2,1)S(1)} async-done(((bf16[2,512,512]{2,0,1:T(2,128)(2,1)}), bf16[2,512,512]{2,0,1:T(2,128)(2,1)S(1)}, u32[]{:S(2)}, u32[]{:S(2)}) %all-to-all-start) | async-done | bytes 1048608 | tf_op jit(solution)/shard_map/all_to_all | solution.py:80
  71.0 5.9 %convolution_bitcast_fusion = f32[256,2048]{1,0:T(8,128)S(1)} fusion(bf16[256,2048]{1,0:T(8,128)(2,1)S(1)} %bitcast.77, bf16[2048,2048]{1,0:T(8,128)(2,1)} %copy-done.2), kind=kOutput, calls=%fused_computation.69 | convolution fusion | flops 2147483648 | bytes 11534336 | tf_op jit(solution)/shard_map/dot_general | solution.py:60
  76.9 5.9 %convolution_bitcast_fusion.1 = f32[256,2048]{1,0:T(8,128)S(1)} fusion(bf16[256,2048]{1,0:T(8,128)(2,1)S(1)} %bitcast.78, bf16[2048,2048]{1,0:T(8,128)(2,1)} %fusion.102), kind=kOutput, calls=%fused_computation.70 | convolution fusion | flops 2147483648 | bytes 11534336 | tf_op jit(solution)/shard_map/dot_general | solution.py:60
  82.8 1.2 fusion.16
  84.0 1.1 fusion.18
  85.2 2.4 %fusion.43 = f32[256,2048]{1,0:T(8,128)S(1)} fusion(bf16[2048,2048]{1,0:T(8,128)(2,1)S(1)} %bitcast.82, bf16[128,2048]{1,0:T(8,128)(2,1)S(1)} %fusion.18, bf16[128,2048]{1,0:T(8,128)(2,1)S(1)} %get-tuple-element.8), kind=kOutput, calls=%fused_computation.147 | convolution fusion | flops 2149580800 | bytes 11534336 | tf_op jit(solution)/shard_map/dot_general | solution.py:60
  87.6 5.7 %fusion.44 = f32[256,2048]{1,0:T(8,128)S(1)} fusion(bf16[2048,2048]{1,0:T(8,128)(2,1)} %fusion.102, bf16[128,2048]{1,0:T(8,128)(2,1)S(1)} %fusion.18, bf16[128,2048]{1,0:T(8,128)(2,1)S(1)} %get-tuple-element.8), kind=kOutput, calls=%fused_computation.148 | convolution fusion | flops 2149580800 | bytes 11534336 | tf_op jit(solution)/shard_map/dot_general | solution.py:60
  93.3 1.4 %fusion.20 = (bf16[128,2048]{1,0:T(8,128)(2,1)S(1)}, bf16[128,2048]{1,0:T(8,128)(2,1)S(1)}, bf16[128,2048]{1,0:T(8,128)(2,1)S(1)}) fusion(f32[128,2048]{1,0:T(8,128)S(1)} %bitcast.71, f32[256,2048]{1,0:T(8,128)S(1)} %fusion.44, f32[256,2048]{1,0:T(8,128)S(1)} %fusion.43), kind=kLoop, calls=%fused_computation.101 | loop fusion | flops 9961472 | bytes 6815744 | tf_op jit(solution)/shard_map/convert_element_type | solution.py:92
  94.7 1.1 fusion.22
  95.9 3.4 %fusion.6 = f32[256,512]{1,0:T(8,128)S(1)} fusion(s32[512]{0:T(512)S(1)} %broadcast_add_fusion.1, s32[2048]{0:T(1024)S(1)} %broadcast_add_fusion, bf16[128,2048]{1,0:T(8,128)(2,1)S(1)} %fusion.22, bf16[128,2048]{1,0:T(8,128)(2,1)S(1)} %get-tuple-element.5), kind=kOutput, calls=%fused_computation.71 | convolution fusion | flops 562036736 | bytes 1583104 | tf_op jit(solution)/shard_map/dot_general | solution.py:60
  99.3 5.0 %fusion.8 = f32[256,512]{1,0:T(8,128)S(1)} fusion(s32[512]{0:T(512)S(1)} %broadcast_add_fusion.1, s32[2048]{0:T(1024)S(1)} %broadcast_add_fusion, bf16[128,2048]{1,0:T(8,128)(2,1)S(1)} %fusion.22, bf16[128,2048]{1,0:T(8,128)(2,1)S(1)} %get-tuple-element.5), kind=kOutput, calls=%fused_computation.72 | convolution fusion | flops 576716800 | bytes 1583104 | tf_op jit(solution)/shard_map/dot_general | solution.py:60
  105.5 3.7 %all-to-all-start.3 = ((bf16[32,2,16,128]{3,2,1,0:T(8,128)(2,1)}), bf16[32,2,16,128]{3,2,1,0:T(8,128)(2,1)S(1)}, u32[]{:S(2)}, u32[]{:S(2)}) async-start(bf16[32,2,16,128]{3,2,1,0:T(8,128)(2,1)} %copy.20), calls=%async_computation.3 | async-start | bytes 524288 | tf_op jit(solution)/shard_map/all_to_all | solution.py:100
  109.3 10.1 %all-to-all-done.3 = bf16[32,2,16,128]{3,2,1,0:T(8,128)(2,1)S(1)} async-done(((bf16[32,2,16,128]{3,2,1,0:T(8,128)(2,1)}), bf16[32,2,16,128]{3,2,1,0:T(8,128)(2,1)S(1)}, u32[]{:S(2)}, u32[]{:S(2)}) %all-to-all-start.3) | async-done | bytes 262176 | tf_op jit(solution)/shard_map/all_to_all | solution.py:100
  (64 shorter events, 12.2 us)
Async XLA Ops:
  2.8 20.8 %all-to-all-start.1 = ((bf16[4,128,512]{2,1,0:T(8,128)(2,1)}), bf16[4,128,512]{2,1,0:T(8,128)(2,1)S(1)}, u32[]{:S(2)}, u32[]{:S(2)}) async-start(bf16[4,128,512]{2,1,0:T(8,128)(2,1)} %bitcast.6), calls=%async_computation.1 | async-start | bytes 1048576 | tf_op jit(solution)/shard_map/all_to_all | solution.py:81
  11.3 7.3 %copy-start.2 = (bf16[2048,2048]{1,0:T(8,128)(2,1)}, bf16[2048,2048]{1,0:T(8,128)(2,1)S(1)}, u32[]{:S(2)}) copy-start(bf16[2048,2048]{1,0:T(8,128)(2,1)S(1)} %fusion.101) | copy-start | bytes 25165828
  13.6 13.6 %copy-start.1 = (bf16[2,512,512]{2,1,0:T(8,128)(2,1)S(1)}, bf16[2,512,512]{2,1,0:T(8,128)(2,1)}, u32[]{:S(2)}) copy-start(bf16[2,512,512]{2,1,0:T(8,128)(2,1)} %param.2) | copy-start | bytes 3145732
  23.6 17.5 %all-to-all-start.2 = ((bf16[4,128,512]{2,1,0:T(8,128)(2,1)}), bf16[4,128,512]{2,1,0:T(8,128)(2,1)S(1)}, u32[]{:S(2)}, u32[]{:S(2)}) async-start(bf16[4,128,512]{2,1,0:T(8,128)(2,1)} %bitcast.8), calls=%async_computation.2 | async-start | bytes 1048576 | tf_op jit(solution)/shard_map/all_to_all | solution.py:81
  41.1 7.1 %copy-start = (bf16[4,128,512]{2,1,0:T(8,128)(2,1)}, bf16[4,128,512]{2,1,0:T(8,128)(2,1)S(1)}, u32[]{:S(2)}) copy-start(bf16[4,128,512]{2,1,0:T(8,128)(2,1)S(1)} %all-to-all-done.2) | copy-start | bytes 1572868
  41.1 28.8 %all-to-all-start = ((bf16[2,512,512]{2,0,1:T(2,128)(2,1)}), bf16[2,512,512]{2,0,1:T(2,128)(2,1)S(1)}, u32[]{:S(2)}, u32[]{:S(2)}) async-start(bf16[2,512,512]{2,0,1:T(2,128)(2,1)} %copy.14), calls=%async_computation | async-start | bytes 2097152 | tf_op jit(solution)/shard_map/all_to_all | solution.py:80
  71.0 14.2 %slice-start = ((s8[8388608]{0:T(1024)(128)(4,1)}), s8[4194304]{0:T(1024)(128)(4,1)S(1)}, s32[]{:S(2)}) async-start(s8[8388608]{0:T(1024)(128)(4,1)} %bitcast.81), calls=%async_computation.4 | async-start | bytes 8388608
  76.9 8.3 %slice-start.1 = ((s8[8388608]{0:T(1024)(128)(4,1)}), s8[4194304]{0:T(1024)(128)(4,1)S(1)}, s32[]{:S(2)}) async-start(s8[8388608]{0:T(1024)(128)(4,1)} %bitcast.81), calls=%async_computation.5 | async-start | bytes 8388608
  105.5 13.9 %all-to-all-start.3 = ((bf16[32,2,16,128]{3,2,1,0:T(8,128)(2,1)}), bf16[32,2,16,128]{3,2,1,0:T(8,128)(2,1)S(1)}, u32[]{:S(2)}, u32[]{:S(2)}) async-start(bf16[32,2,16,128]{3,2,1,0:T(8,128)(2,1)} %copy.20), calls=%async_computation.3 | async-start | bytes 524288 | tf_op jit(solution)/shard_map/all_to_all | solution.py:100
where the time goes:
time: 124 us; the launch traced here: 123 us
  waiting for transfers between devices  43.7 us (35%)
  matrix products  31.3 us (25%)
  other arithmetic  25.2 us (20%)
  starting transfers between devices  17.2 us (14%)
  local copies, waits for them, and re-layouts  5.58 us (4%)
    dot_general x6, matrix products, matmul(): return jnp.dot(left, right, preferred_element_type=jnp.float32)  28.3 us
    all_to_all x1, waiting for transfers between devices, on_device(): lax.all_to_all(near_field, 'grp', split_axis=1, concat_axis=2, tiled=True)  20.1 us
    unnamed x31, other arithmetic  14.3 us
    all_to_all x2, waiting for transfers between devices, on_device(): lax.all_to_all(part, 'grp', split_axis=0, concat_axis=1, tiled=True)  13.5 us
    all_to_all x1, waiting for transfers between devices, on_device(): lax.all_to_all(cols, ('slab', 'grp'), split_axis=0, concat_axis=0, tiled=...  10.1 us
    all_to_all x2, starting transfers between devices, on_device(): lax.all_to_all(part, 'grp', split_axis=0, concat_axis=1, tiled=True)  9.82 us
    all_to_all x1, starting transfers between devices, on_device(): lax.all_to_all(cols, ('slab', 'grp'), split_axis=0, concat_axis=0, tiled=...  3.71 us
    all_to_all x1, starting transfers between devices, on_device(): lax.all_to_all(near_field, 'grp', split_axis=1, concat_axis=2, tiled=True)  3.7 us
  transfers between devices with their start and end apart: 4, of which 4 were waited for; matrix products, arithmetic and copies ran while one was open for 16% of the time, Pallas kernels for 0%

commit v1 on v0

--- a/solution.py
+++ b/solution.py
@@ -77,7 +77,16 @@
     rows = lat_dev // group_count
     angles = AV // devices
     coded = [jnp.exp2(lens_phase[k] * PHASE_CODE).astype(jnp.bfloat16) for k in range(steps)]
-    field = lax.all_to_all(near_field, "grp", split_axis=1, concat_axis=2, tiled=True)
+
+    def pools_do(local_array, axis_no, dim_at):
+        work_now = lax.psum(1, "grp")
+        placed = jnp.split(local_array, work_now, dim_at)
+        formed = jnp.concatenate(
+            lax.all_to_all(jnp.stack(placed), "grp", split_axis=0, concat_axis=0), axis=axis_no
+        )
+        return formed
+
+    field = pools_do(near_field, 2, 1)
     coded = [lax.all_to_all(part, "grp", split_axis=0, concat_axis=1, tiled=True) for part in coded]
     prop_cos, prop_sin = propagator(points)
     both = field.reshape(2 * rows, points)

time: 124 us -> 117 us (0.944)
  matrix products: 31.3 us -> 24.5 us
  other arithmetic: 25.2 us -> 19.3 us
  local copies, waits for them, and re-layouts: 5.58 us -> 9.2 us
  waiting for transfers between devices: 43.7 us -> 45.9 us
    unnamed x31 -> x32, other arithmetic: 14.3 us -> 7.27 us
    dot_general x6, matrix products: 28.3 us -> 21.5 us  [matmul(): return jnp.dot(left, right, preferred_element_type=jnp.float32)]
    unnamed x14 -> x19, local copies, waits for them, and re-layouts: 3.35 us -> 6.86 us
    all_to_all x2, waiting for transfers between devices: 13.5 us -> 15.6 us  [on_device(): lax.all_to_all(part, 'grp', split_axis=0, concat_axis=1, tiled=True)]
  transfers between devices with their start and end apart: 4 -> 4, of which waited for: 4 -> 4; matrix products, arithmetic and copies ran while one was open for 16% -> 10% of each run, Pallas kernels for 0% -> 0%
where the time goes in v1:
time: 117 us
  waiting for transfers between devices  45.9 us (39%)
  matrix products  24.5 us (21%)
  other arithmetic  19.3 us (16%)
  starting transfers between devices  17.2 us (15%)
  local copies, waits for them, and re-layouts  9.2 us (8%)
    dot_general x6, matrix products, matmul(): return jnp.dot(left, right, preferred_element_type=jnp.float32)  21.5 us
    all_to_all x1, waiting for transfers between devices, pools_do(): lax.all_to_all(jnp.stack(placed), 'grp', split_axis=0, concat_axis=0)  20.1 us
    all_to_all x2, waiting for transfers between devices, on_device(): lax.all_to_all(part, 'grp', split_axis=0, concat_axis=1, tiled=True)  15.6 us
    all_to_all x1, waiting for transfers between devices, on_device(): lax.all_to_all(cols, ('slab', 'grp'), split_axis=0, concat_axis=0, tiled=...  10.1 us
    all_to_all x2, starting transfers between devices, on_device(): lax.all_to_all(part, 'grp', split_axis=0, concat_axis=1, tiled=True)  9.82 us
    unnamed x32, other arithmetic  7.27 us
    unnamed x19, local copies, waits for them, and re-layouts  6.86 us
    all_to_all x1, starting transfers between devices, on_device(): lax.all_to_all(cols, ('slab', 'grp'), split_axis=0, concat_axis=0, tiled=...  3.71 us
  transfers between devices with their start and end apart: 4, of which 4 were waited for; matrix products, arithmetic and copies ran while one was open for 10% of the time, Pallas kernels for 0%

profile of v1, /device:TPU:0, one launch (start us, length us, event | category | flops | bytes accessed | tf_op | source)
XLA Modules:
  0.0 116.6 jit_solution(632398541088401806)
XLA Ops:
  0.0 2.8 %exponential_convert_fusion.1 = (bf16[1,512,512]{2,1,0:T(8,128)(2,1)}, bf16[1,512,512]{2,1,0:T(8,128)(2,1)}) fusion(f32[2,512,512]{2,1,0:T(8,128)} %param.3), kind=kLoop, calls=%fused_computation.137 | loop fusion | flops 1048576 | bytes 3145728 | tf_op jit(solution)/shard_map/convert_element_type | solution.py:79
  2.8 6.3 %all-to-all-start.1 = ((bf16[4,128,512]{2,1,0:T(8,128)(2,1)}), bf16[4,128,512]{2,1,0:T(8,128)(2,1)S(1)}, u32[]{:S(2)}, u32[]{:S(2)}) async-start(bf16[4,128,512]{2,1,0:T(8,128)(2,1)} %bitcast.7), calls=%async_computation.1 | async-start | bytes 1048576 | tf_op jit(solution)/shard_map/all_to_all | solution.py:90
  9.2 1.4 %fusion.27 = (bf16[128,2048]{1,0:T(8,128)(2,1)S(1)}, bf16[128,2048]{1,0:T(8,128)(2,1)S(1)}) fusion(s32[128]{0:T(128)S(1)} %iota.18, s32[2048]{0:T(1024)S(1)} %iota.21), kind=kLoop, calls=%fused_computation.106 | loop fusion | flops 10223616 | bytes 1057280 | tf_op jit(solution)/shard_map/convert_element_type | solution.py:47
  11.3 3.3 %copy-done.2 = bf16[2048,2048]{1,0:T(8,128)(2,1)} copy-done((bf16[2048,2048]{1,0:T(8,128)(2,1)}, bf16[2048,2048]{1,0:T(8,128)(2,1)S(1)}, u32[]{:S(2)}) %copy-start.2) | copy-done | bytes 8388632
  15.0 3.2 %copy-done.3 = bf16[2048,2048]{1,0:T(8,128)(2,1)} copy-done((bf16[2048,2048]{1,0:T(8,128)(2,1)}, bf16[2048,2048]{1,0:T(8,128)(2,1)S(1)}, u32[]{:S(2)}) %copy-start.3) | copy-done | bytes 8388632
  18.3 5.3 %all-to-all-done.1 = bf16[4,128,512]{2,1,0:T(8,128)(2,1)S(1)} async-done(((bf16[4,128,512]{2,1,0:T(8,128)(2,1)}), bf16[4,128,512]{2,1,0:T(8,128)(2,1)S(1)}, u32[]{:S(2)}, u32[]{:S(2)}) %all-to-all-start.1) | async-done | bytes 524320 | tf_op jit(solution)/shard_map/all_to_all | solution.py:90
  23.6 3.5 %all-to-all-start.2 = ((bf16[4,128,512]{2,1,0:T(8,128)(2,1)}), bf16[4,128,512]{2,1,0:T(8,128)(2,1)S(1)}, u32[]{:S(2)}, u32[]{:S(2)}) async-start(bf16[4,128,512]{2,1,0:T(8,128)(2,1)} %bitcast.9), calls=%async_computation.2 | async-start | bytes 1048576 | tf_op jit(solution)/shard_map/all_to_all | solution.py:90
  27.1 1.1 pad_maximum_fusion
  28.2 0.8 fusion.92
  29.1 0.8 fusion.94
  29.9 0.9 fusion.96
  30.8 10.3 %all-to-all-done.2 = bf16[4,128,512]{2,1,0:T(8,128)(2,1)S(1)} async-done(((bf16[4,128,512]{2,1,0:T(8,128)(2,1)}), bf16[4,128,512]{2,1,0:T(8,128)(2,1)S(1)}, u32[]{:S(2)}, u32[]{:S(2)}) %all-to-all-start.2) | async-done | bytes 524320 | tf_op jit(solution)/shard_map/all_to_all | solution.py:90
  41.1 3.7 %all-to-all-start = ((bf16[4,2,128,512]{3,2,1,0:T(8,128)(2,1)}), bf16[4,2,128,512]{3,2,1,0:T(8,128)(2,1)S(1)}, u32[]{:S(2)}, u32[]{:S(2)}) async-start(bf16[4,2,128,512]{3,2,1,0:T(8,128)(2,1)} %pad_maximum_fusion), calls=%async_computation | async-start | bytes 2097152 | tf_op jit(solution)/shard_map/all_to_all | solution.py:85
  44.9 0.8 fusion.98
  45.7 0.8 fusion.100
  46.5 0.8 fusion.74
  47.4 0.8 fusion.102
  48.5 1.2 %multiply_bitcast_fusion = f32[4,16,8,512]{3,2,1,0:T(8,128)S(1)} fusion(bf16[4,128,512]{2,1,0:T(8,128)(2,1)} %copy-done), kind=kLoop, calls=%fused_computation.127 | loop fusion | flops 524288 | bytes 1572864
  49.8 20.1 %all-to-all-done = bf16[4,2,128,512]{3,2,1,0:T(8,128)(2,1)S(1)} async-done(((bf16[4,2,128,512]{3,2,1,0:T(8,128)(2,1)}), bf16[4,2,128,512]{3,2,1,0:T(8,128)(2,1)S(1)}, u32[]{:S(2)}, u32[]{:S(2)}) %all-to-all-start) | async-done | bytes 1048608 | tf_op jit(solution)/shard_map/all_to_all | solution.py:85
  69.9 0.8 copy.14
  71.0 5.9 %fusion.293 = f32[256,2048]{1,0:T(8,128)S(1)} fusion(bf16[256,2048]{1,0:T(8,128)(2,1)S(1)} %bitcast.80, bf16[2048,2048]{1,0:T(8,128)(2,1)} %copy-done.2), kind=kOutput, calls=%fused_computation.423 | convolution fusion | flops 2147483648 | bytes 11534336 | tf_op jit(solution)/shard_map/dot_general | solution.py:60
  77.0 2.4 %fusion.292 = f32[256,2048]{1,0:T(8,128)S(1)} fusion(bf16[256,2048]{1,0:T(8,128)(2,1)S(1)} %bitcast.81, bf16[2048,2048]{1,0:T(8,128)(2,1)S(1)} %bitcast.87), kind=kOutput, calls=%fused_computation.422 | convolution fusion | flops 2147483648 | bytes 11534336 | tf_op jit(solution)/shard_map/dot_general | solution.py:60
  79.4 1.2 %fusion.16 = (bf16[128,2048]{1,0:T(8,128)(2,1)S(1)}, bf16[128,2048]{1,0:T(8,128)(2,1)S(1)}, bf16[128,2048]{1,0:T(8,128)(2,1)S(1)}) fusion(f32[128,2048]{1,0:T(8,128)S(1)} %bitcast.76, f32[256,2048]{1,0:T(8,128)S(1)} %fusion.292, f32[256,2048]{1,0:T(8,128)S(1)} %fusion.293), kind=kLoop, calls=%fused_computation.95 | loop fusion | flops 9961472 | bytes 6815744 | tf_op jit(solution)/shard_map/convert_element_type | solution.py:101
  80.6 1.1 fusion.18
  81.7 2.4 %fusion.43 = f32[256,2048]{1,0:T(8,128)S(1)} fusion(bf16[2048,2048]{1,0:T(8,128)(2,1)S(1)} %bitcast.85, bf16[128,2048]{1,0:T(8,128)(2,1)S(1)} %fusion.18, bf16[128,2048]{1,0:T(8,128)(2,1)S(1)} %get-tuple-element.8), kind=kOutput, calls=%fused_computation.146 | convolution fusion | flops 2149580800 | bytes 11534336 | tf_op jit(solution)/shard_map/dot_general | solution.py:60
  84.1 2.4 %fusion.44 = f32[256,2048]{1,0:T(8,128)S(1)} fusion(bf16[2048,2048]{1,0:T(8,128)(2,1)S(1)} %bitcast.87, bf16[128,2048]{1,0:T(8,128)(2,1)S(1)} %fusion.18, bf16[128,2048]{1,0:T(8,128)(2,1)S(1)} %get-tuple-element.8), kind=kOutput, calls=%fused_computation.147 | convolution fusion | flops 2149580800 | bytes 11534336 | tf_op jit(solution)/shard_map/dot_general | solution.py:60
  86.5 1.4 %fusion.20 = (bf16[128,2048]{1,0:T(8,128)(2,1)S(1)}, bf16[128,2048]{1,0:T(8,128)(2,1)S(1)}, bf16[128,2048]{1,0:T(8,128)(2,1)S(1)}) fusion(f32[128,2048]{1,0:T(8,128)S(1)} %bitcast.74, f32[256,2048]{1,0:T(8,128)S(1)} %fusion.44, f32[256,2048]{1,0:T(8,128)S(1)} %fusion.43), kind=kLoop, calls=%fused_computation.99 | loop fusion | flops 9961472 | bytes 6815744 | tf_op jit(solution)/shard_map/convert_element_type | solution.py:101
  88.0 1.1 fusion.22
  89.1 3.4 %fusion.6 = f32[256,512]{1,0:T(8,128)S(1)} fusion(s32[512]{0:T(512)S(1)} %broadcast_add_fusion.1, s32[2048]{0:T(1024)S(1)} %broadcast_add_fusion, bf16[128,2048]{1,0:T(8,128)(2,1)S(1)} %fusion.22, bf16[128,2048]{1,0:T(8,128)(2,1)S(1)} %get-tuple-element.5), kind=kOutput, calls=%fused_computation.69 | convolution fusion | flops 562036736 | bytes 1583104 | tf_op jit(solution)/shard_map/dot_general | solution.py:60
  92.5 5.0 %fusion.8 = f32[256,512]{1,0:T(8,128)S(1)} fusion(s32[512]{0:T(512)S(1)} %broadcast_add_fusion.1, s32[2048]{0:T(1024)S(1)} %broadcast_add_fusion, bf16[128,2048]{1,0:T(8,128)(2,1)S(1)} %fusion.22, bf16[128,2048]{1,0:T(8,128)(2,1)S(1)} %get-tuple-element.5), kind=kOutput, calls=%fused_computation.70 | convolution fusion | flops 576716800 | bytes 1583104 | tf_op jit(solution)/shard_map/dot_general | solution.py:60
  98.7 3.7 %all-to-all-start.3 = ((bf16[32,2,16,128]{3,2,1,0:T(8,128)(2,1)}), bf16[32,2,16,128]{3,2,1,0:T(8,128)(2,1)S(1)}, u32[]{:S(2)}, u32[]{:S(2)}) async-start(bf16[32,2,16,128]{3,2,1,0:T(8,128)(2,1)} %copy.19), calls=%async_computation.3 | async-start | bytes 524288 | tf_op jit(solution)/shard_map/all_to_all | solution.py:109
  102.5 10.1 %all-to-all-done.3 = bf16[32,2,16,128]{3,2,1,0:T(8,128)(2,1)S(1)} async-done(((bf16[32,2,16,128]{3,2,1,0:T(8,128)(2,1)}), bf16[32,2,16,128]{3,2,1,0:T(8,128)(2,1)S(1)}, u32[]{:S(2)}, u32[]{:S(2)}) %all-to-all-start.3) | async-done | bytes 262176 | tf_op jit(solution)/shard_map/all_to_all | solution.py:109
  (72 shorter events, 6.9 us)
Async XLA Ops:
  2.8 20.8 %all-to-all-start.1 = ((bf16[4,128,512]{2,1,0:T(8,128)(2,1)}), bf16[4,128,512]{2,1,0:T(8,128)(2,1)S(1)}, u32[]{:S(2)}, u32[]{:S(2)}) async-start(bf16[4,128,512]{2,1,0:T(8,128)(2,1)} %bitcast.7), calls=%async_computation.1 | async-start | bytes 1048576 | tf_op jit(solution)/shard_map/all_to_all | solution.py:90
  11.3 3.3 %copy-start.2 = (bf16[2048,2048]{1,0:T(8,128)(2,1)}, bf16[2048,2048]{1,0:T(8,128)(2,1)S(1)}, u32[]{:S(2)}) copy-start(bf16[2048,2048]{1,0:T(8,128)(2,1)S(1)} %fusion.101) | copy-start | bytes 25165828
  14.6 3.6 %copy-start.1 = (bf16[2,512,512]{2,1,0:T(8,128)(2,1)S(1)}, bf16[2,512,512]{2,1,0:T(8,128)(2,1)}, u32[]{:S(2)}) copy-start(bf16[2,512,512]{2,1,0:T(8,128)(2,1)} %param.2) | copy-start | bytes 3145732
  15.0 3.2 %copy-start.3 = (bf16[2048,2048]{1,0:T(8,128)(2,1)}, bf16[2048,2048]{1,0:T(8,128)(2,1)S(1)}, u32[]{:S(2)}) copy-start(bf16[2048,2048]{1,0:T(8,128)(2,1)S(1)} %fusion.90) | copy-start | bytes 25165828
  23.6 17.5 %all-to-all-start.2 = ((bf16[4,128,512]{2,1,0:T(8,128)(2,1)}), bf16[4,128,512]{2,1,0:T(8,128)(2,1)S(1)}, u32[]{:S(2)}, u32[]{:S(2)}) async-start(bf16[4,128,512]{2,1,0:T(8,128)(2,1)} %bitcast.9), calls=%async_computation.2 | async-start | bytes 1048576 | tf_op jit(solution)/shard_map/all_to_all | solution.py:90
  41.1 7.1 %copy-start = (bf16[4,128,512]{2,1,0:T(8,128)(2,1)}, bf16[4,128,512]{2,1,0:T(8,128)(2,1)S(1)}, u32[]{:S(2)}) copy-start(bf16[4,128,512]{2,1,0:T(8,128)(2,1)S(1)} %all-to-all-done.2) | copy-start | bytes 1572868
  41.1 28.8 %all-to-all-start = ((bf16[4,2,128,512]{3,2,1,0:T(8,128)(2,1)}), bf16[4,2,128,512]{3,2,1,0:T(8,128)(2,1)S(1)}, u32[]{:S(2)}, u32[]{:S(2)}) async-start(bf16[4,2,128,512]{3,2,1,0:T(8,128)(2,1)} %pad_maximum_fusion), calls=%async_computation | async-start | bytes 2097152 | tf_op jit(solution)/shard_map/all_to_all | solution.py:85
  70.7 6.2 %slice-start.2 = ((s8[8388608]{0:T(1024)(128)(4,1)}), s8[4194304]{0:T(1024)(128)(4,1)S(1)}, s32[]{:S(2)}) async-start(s8[8388608]{0:T(1024)(128)(4,1)} %bitcast.86), calls=%async_computation.6 | async-start | bytes 8388608
  71.0 5.9 %slice-start.3 = ((s8[8388608]{0:T(1024)(128)(4,1)}), s8[4194304]{0:T(1024)(128)(4,1)S(1)}, s32[]{:S(2)}) async-start(s8[8388608]{0:T(1024)(128)(4,1)} %bitcast.86), calls=%async_computation.7 | async-start | bytes 8388608
  71.0 10.7 %slice-start = ((s8[8388608]{0:T(1024)(128)(4,1)}), s8[4194304]{0:T(1024)(128)(4,1)S(1)}, s32[]{:S(2)}) async-start(s8[8388608]{0:T(1024)(128)(4,1)} %bitcast.84), calls=%async_computation.4 | async-start | bytes 8388608
  77.0 4.8 %slice-start.1 = ((s8[8388608]{0:T(1024)(128)(4,1)}), s8[4194304]{0:T(1024)(128)(4,1)S(1)}, s32[]{:S(2)}) async-start(s8[8388608]{0:T(1024)(128)(4,1)} %bitcast.84), calls=%async_computation.5 | async-start | bytes 8388608
  98.7 13.9 %all-to-all-start.3 = ((bf16[32,2,16,128]{3,2,1,0:T(8,128)(2,1)}), bf16[32,2,16,128]{3,2,1,0:T(8,128)(2,1)S(1)}, u32[]{:S(2)}, u32[]{:S(2)}) async-start(bf16[32,2,16,128]{3,2,1,0:T(8,128)(2,1)} %copy.19), calls=%async_computation.3 | async-start | bytes 524288 | tf_op jit(solution)/shard_map/all_to_all | solution.py:109
